TPU v7x, 32 devices: a whole 2x2x4 slice. The times are simulated.
32 devices in a mesh: gx: 16 (over z, x, core), gy: 2 (over y).
Axes of the slice: x: 2, y: 2, z: 4, core: 2. Of those that a mesh axis runs over, the one named last changes fastest.
Arguments:
- particles: float32 [64, 2, 64, 1024], P(None, None, 'gx', 'gy'), may hold values from -32 to 32, as said below
- background: float32 [2, 64, 1024], P(None, 'gx', 'gy'), may hold values from -6 to 6
- obs_tile: int32 [16, 256], P('gx', 'gy'), may hold values from 0 to 127
- obs_mask: int32 [16, 16, 256], P(None, 'gx', 'gy'), may hold values 0 or 1
- obs_value: float32 [16, 256], P('gx', 'gy'), may hold values from -6 to 6
- obs_var: float32 [16, 256], P('gx', 'gy'), may hold values from 0.1 to 1
Outputs:
- analysis: float32 [64, 2, 64, 1024], P(None, None, 'gx', 'gy')
Inputs may be any that keep to these rules, and one draw needn't show every extreme that they name: `particles`: each particle is a field of order one to a few. `obs_tile`: an observation's value names tile row t // 128 and tile column t % (128) of its slab.
All inputs are finite; a program needn't handle non-finite values. No bound on the sum of `obs_mask` on one device may be relied on, other than what follows from the above.
Results may differ from a plain program's by a relative error of at most 0.0001.
Values sent between devices are 32-bit elements; how exact they have to be, the bound alone decides.
A program may use at most 64 MiB of HBM per device.

v0:
```python
import jax
import jax.numpy as jnp
from jax import lax
from jax.sharding import PartitionSpec as P

STEPS = 2
TILE = 4


lap_weight = 0.25
prior_weight = 0.05
couple_weight = 0.5
step_length = 1.0
epsilon = 1e-06
highest = lax.Precision.HIGHEST


def with_halo(block, sides, width):
    for axis, dim in sides:
        count = lax.axis_size(axis)
        forward = [(i, i + 1) for i in range(count - 1)]
        forward.append((count - 1, 0))
        backward = [(target, source) for source, target in forward]
        low = lax.ppermute(
            lax.slice_in_dim(block, block.shape[dim] - width, None, axis=dim), axis, forward
        )
        high = lax.ppermute(lax.slice_in_dim(block, 0, width, axis=dim), axis, backward)
        block = jnp.concatenate([low, block, high], axis=dim)
    return block


def laplace_inner(field):
    total = field[..., 1:-1, 2:] + field[..., 1:-1, :-2]
    total = total + field[..., 2:, 1:-1] + field[..., :-2, 1:-1]
    return total - 4.0 * field[..., 1:-1, 1:-1]


def prior_term(deviation):
    padded = with_halo(deviation, (("gx", 2), ("gy", 3)), 2)
    smooth = padded[..., 1:-1, 1:-1] - lap_weight * laplace_inner(padded)
    curved = smooth[..., 1:-1, 1:-1] - lap_weight * laplace_inner(smooth)
    return -prior_weight * (curved + couple_weight * (deviation - deviation[:, ::-1]))


def observe_term(state, table, weights, values, variance):
    count, rows, cols = (state.shape[0], state.shape[2], state.shape[3])
    tile_rows, tile_cols = (rows // TILE, cols // TILE)
    upper = state[:, 0].reshape(count, tile_rows, TILE, tile_cols, TILE)
    cells = upper.transpose(2, 4, 0, 1, 3).reshape(TILE * TILE, count, tile_rows * tile_cols)
    picked = jnp.einsum("cpt,ot->cpo", cells, table, precision=highest)
    mapped = 0.25 * jnp.sum(weights[:, None, :] * picked, axis=0)
    innovation = (values[None, :] - mapped) / variance[None, :]
    contrib = (0.25 * weights)[:, None, :] * innovation[None]
    spread = jnp.einsum("cpo,ot->cpt", contrib, table, precision=highest)
    back = spread.reshape(TILE, TILE, count, tile_rows, tile_cols).transpose(2, 3, 0, 4, 1)
    back = back.reshape(count, rows, cols)
    return jnp.stack([back, jnp.zeros_like(back)], axis=1)


def norm_scale(drift, denominator):
    total = lax.psum(jnp.sum(drift * drift), ("gx", "gy"))
    return step_length / jnp.sqrt(total / denominator + epsilon)


def per_device(particles, background, obs_tile, obs_mask, obs_value, obs_var):
    count = particles.shape[0]
    tiles = particles.shape[2] // TILE * (particles.shape[3] // TILE)
    table = (obs_tile[0][:, None] == jnp.arange(tiles, dtype=jnp.int32)[None, :]).astype(
        jnp.float32
    )
    weights = obs_mask[:, 0, :].astype(jnp.float32)
    values = obs_value[0]
    variance = obs_var[0]
    local_size = particles[0].size
    total_size = float(local_size * lax.axis_size("gx") * lax.axis_size("gy"))
    pair_count = float(count * (count - 1))
    off_diag = 1.0 - jnp.eye(count, dtype=jnp.float32)
    state = particles
    gram = None
    for step in range(STEPS):
        deviation = state - background[None]
        flat_dev = deviation.reshape(count, -1)
        if gram is None:
            gram = lax.psum(jnp.dot(flat_dev, flat_dev.T, precision=highest), ("gx", "gy"))
        gradient = prior_term(deviation) + observe_term(state, table, weights, values, variance)
        flat_grad = gradient.reshape(count, -1)
        diagonal = jnp.diagonal(gram)
        distance = diagonal[:, None] + diagonal[None, :] - 2.0 * gram
        width = jnp.sum(distance * off_diag) / (pair_count * total_size) + epsilon
        kernel = jnp.exp(-distance / (2.0 * width * total_size))
        attract = jnp.dot(kernel, flat_grad, precision=highest)
        pulled = jnp.dot(kernel, flat_dev, precision=highest)
        drift = (attract + (jnp.sum(kernel, axis=1)[:, None] * flat_dev - pulled) / width) / count
        if step + 1 < STEPS:
            cross, square = lax.psum(
                (
                    jnp.dot(flat_dev, drift.T, precision=highest),
                    jnp.dot(drift, drift.T, precision=highest),
                ),
                ("gx", "gy"),
            )
            scale = step_length / jnp.sqrt(jnp.trace(square) / (count * total_size) + epsilon)
            gram = gram + scale * (cross + cross.T) + scale * scale * square
        else:
            scale = norm_scale(drift, count * total_size)
        state = state + scale * drift.reshape(state.shape)
    return state


def solution(mesh):
    return jax.shard_map(
        per_device,
        mesh=mesh,
        in_specs=(
            P(None, None, "gx", "gy"),
            P(None, "gx", "gy"),
            P("gx", "gy"),
            P(None, "gx", "gy"),
            P("gx", "gy"),
            P("gx", "gy"),
        ),
        out_specs=P(None, None, "gx", "gy"),
        check_vma=False,
    )
```

profile of v0, /device:TPU:0, one launch (start us, length us, event | category | flops | bytes accessed | tf_op | source)
XLA Modules:
  0.0 222.8 jit_solution(16743643375088304163)
XLA Ops:
  0.0 2.8 %copy.40 = f32[64,2,4,512]{0,3,2,1:T(8,128)} copy(f32[64,2,4,512]{3,2,1,0:T(4,128)} %param.6) | data formatting | bytes 2097152 | tf_op args[0]
  2.8 2.2 broadcast_subtract_fusion.1
  5.0 1.1 fusion.58
  6.1 2.4 %copy.32 = f32[64,2,2,512]{3,0,2,1:T(8,128)} copy(f32[64,2,2,512]{0,3,2,1:T(8,128)} %get-tuple-element.15) | data formatting | bytes 1048576 | tf_op jit(solution)/shard_map/slice | solution.py:25
  9.0 1.1 copy.33
  10.1 5.0 %collective-permute-start.1 = (f32[64,2,2,512]{3,0,2,1:T(8,128)}, f32[64,2,2,512]{3,0,2,1:T(8,128)}, u32[]{:S(2)}, u32[]{:S(2)}) collective-permute-start(f32[64,2,2,512]{3,0,2,1:T(8,128)} %copy.33), channel_id=1, source_target_pairs={{2,0},{4,2},{6,4},{8,6},{10,8},{12,10},{14,12},{16,14},{18,16},{20... | collective-permute-start | bytes 1572872 | tf_op jit(solution)/shard_map/ppermute | solution.py:27
  15.0 1.9 slice.112
  16.9 3.6 %convolution_bitcast_fusion.1 = f32[64,64]{1,0:T(8,128)S(1)} fusion(f32[64,2,4,512]{0,3,2,1:T(8,128)S(1)} %broadcast_subtract_fusion.1), kind=kOutput, calls=%fused_computation.61 | convolution fusion | flops 201326592 | bytes 1064960 | tf_op jit(solution)/shard_map/dot_general | solution.py:84
  20.5 1.4 copy.36
  21.9 1.1 copy.37
  23.0 38.5 %psum.28 = f32[64,64]{1,0:T(8,128)S(1)} all-reduce(f32[64,64]{1,0:T(8,128)S(1)} %convolution_bitcast_fusion.1), channel_id=1, replica_groups=mesh['gx'=16,'gy'=2] {'gx','gy'}, use_global_device_ids=true, to_apply=%region_0.0 | all-reduce | flops 4096 | bytes 32768 | tf_op jit(solution)/shard_map/psum | solution.py:84
  64.5 1.5 fusion.26
  66.1 3.4 %fusion.1 = f32[64,4096]{1,0:T(8,128)} fusion(f32[64,4096]{0,1:T(8,128)S(1)} %bitcast.63, f32[64,4096]{1,0:T(8,128)S(1)} %copy.57, f32[]{:T(128)S(6)} %add.128, f32[64]{0:T(128)S(1)} %fusion.55, f32[64,64]{1,0:T(8,128)S(1)} %psum.28, f32[]{:T(128)S(6)} %mul.175, f32[64]{0:T(128)S(1)} %gather_fusion), kind=kOutput, calls=%fused_computation.6 | convolution fusion | flops 202133504 | bytes 3162632 | tf_op jit(solution)/shard_map/dot_general | solution.py:92
  69.5 1.4 copy.34
  70.9 2.4 %copy.35 = f32[64,2,2,512]{0,3,2,1:T(8,128)} copy(f32[64,2,2,512]{3,0,2,1:T(8,128)} %collective-permute-done.1) | data formatting | bytes 1048576 | tf_op jit(solution)/shard_map/ppermute | solution.py:27
  74.0 2.4 %collective-permute-start.2 = (f32[64,2,8,2]{0,3,2,1:T(2,128)S(1)}, f32[64,2,8,2]{0,3,2,1:T(2,128)S(1)}, u32[]{:S(2)}, u32[]{:S(2)}) collective-permute-start(f32[64,2,8,2]{0,3,2,1:T(2,128)S(1)} %get-tuple-element.11), channel_id=1, source_target_pairs={{0,1},{1,0},{2,3},{3,2},{4,5},{5,4},{6,7},{7,6},{8,9},{9,8},{10,11... | collective-permute-start | bytes 24584 | tf_op jit(solution)/shard_map/ppermute | solution.py:24
  76.5 1.2 fusion.35
  77.7 2.4 %copy.38 = f32[4,4,64,1,128]{2,1,4,0,3:T(4,128)} copy(f32[4,4,64,1,128]{4,2,1,0,3:T(8,128)} %bitcast.78) | data formatting | bytes 1048576 | tf_op jit(solution)/shard_map/reshape | solution.py:55
  80.1 1.7 pad_maximum_fusion
  81.9 2.2 %fusion.8 = f32[64,2,6,514]{0,3,2,1:T(8,128)S(1)} fusion(f32[64,2,8,516]{0,3,2,1:T(8,128)S(1)} %pad_maximum_fusion, f32[64,2,8,2]{0,3,2,1:T(2,128)S(1)} %collective-permute-done.2, f32[64,2,2,512]{0,3,2,1:T(8,128)S(1)} %copy-done.1, f32[64,2,4,512]{0,3,2,1:T(8,128)S(1)} %broadcast_subtract_fusion.1, f32[64,2,2,512]{0,3,2,1:T(8,128)S(1)} %copy.34, ...), kind=kLoop, calls=%fused_computation.25 | loop fusion | flops 5131776 | bytes 8429568 | tf_op jit(solution)/shard_map/sub | solution.py:40
  84.2 1.2 fusion.13
  85.4 2.4 %convolution_add_fusion.1 = f32[64,4096]{1,0:T(8,128)S(1)} fusion(f32[64,4096]{1,0:T(8,128)S(1)} %copy-done.3, f32[64,4096]{0,1:T(8,128)S(1)} %bitcast.67, f32[64,64]{1,0:T(8,128)S(1)} %psum.28, f32[]{:T(128)S(6)} %mul.175, f32[64]{0:T(128)S(1)} %gather_fusion), kind=kOutput, calls=%fused_computation.7 | convolution fusion | flops 201609216 | bytes 3162372 | tf_op jit(solution)/shard_map/dot_general | solution.py:91
  87.8 1.5 fusion.27
  89.4 1.0 fusion.29
  90.4 41.7 %all-reduce.2 = (f32[64,64]{1,0:T(8,128)S(1)}, f32[64,64]{0,1:T(8,128)S(1)}) all-reduce(f32[64,64]{1,0:T(8,128)S(1)} %fusion.29, f32[64,64]{0,1:T(8,128)S(1)} %fusion.27), channel_id=1, replica_groups=mesh['gx'=16,'gy'=2] {'gx','gy'}, use_global_device_ids=true, to_apply=%region_4.5 | all-reduce | flops 8192 | bytes 65536 | tf_op jit(solution)/shard_map/psum | solution.py:95
  133.4 1.9 copy.58
  135.3 3.5 %broadcast_subtract_fusion = (f32[64,2,4,512]{0,3,2,1:T(8,128)S(1)}, f32[64,2,4,512]{0,3,2,1:T(8,128)}) fusion(f32[2,4,512]{2,1,0:T(4,128)S(1)} %copy-done.7, f32[64,2,4,512]{0,3,2,1:T(8,128)} %copy.40, f32[64,2,4,512]{0,3,2,1:T(8,128)} %bitcast.70), kind=kLoop, calls=%fused_computation.63 | loop fusion | flops 524288 | bytes 4210688 | tf_op jit(solution)/shard_map/sub | solution.py:81
  138.8 1.1 fusion.57
  139.9 2.4 %copy.44 = f32[64,2,2,512]{3,0,2,1:T(8,128)} copy(f32[64,2,2,512]{0,3,2,1:T(8,128)} %get-tuple-element.13) | data formatting | bytes 1048576 | tf_op jit(solution)/shard_map/slice | solution.py:25
  142.3 1.1 copy.45
  143.4 4.4 %collective-permute-start.5 = (f32[64,2,2,512]{3,0,2,1:T(8,128)}, f32[64,2,2,512]{3,0,2,1:T(8,128)}, u32[]{:S(2)}, u32[]{:S(2)}) collective-permute-start(f32[64,2,2,512]{3,0,2,1:T(8,128)} %copy.45), channel_id=1, source_target_pairs={{2,0},{4,2},{6,4},{8,6},{10,8},{12,10},{14,12},{16,14},{18,16},{20... | collective-permute-start | bytes 1572872 | tf_op jit(solution)/shard_map/ppermute | solution.py:27
  147.8 1.3 slice.152
  149.1 1.1 copy.48
  150.3 1.5 fusion.25
  154.8 3.4 %fusion = f32[64,4096]{1,0:T(8,128)} fusion(f32[64,4096]{0,1:T(8,128)S(1)} %bitcast.66, f32[64,4096]{1,0:T(8,128)S(1)} %copy.59, f32[]{:T(128)S(6)} %add.146, f32[64]{0:T(128)S(1)} %fusion.56, f32[64,64]{1,0:T(8,128)S(1)} %fusion.48, f32[]{:T(128)S(6)} %mul.204, f32[64]{0:T(128)S(1)} %gather_fusion.1), kind=kOutput, calls=%fused_computation.3 | convolution fusion | flops 202133504 | bytes 3162632 | tf_op jit(solution)/shard_map/dot_general | solution.py:92
  158.3 1.4 copy.46
  159.6 2.4 %copy.47 = f32[64,2,2,512]{0,3,2,1:T(8,128)} copy(f32[64,2,2,512]{3,0,2,1:T(8,128)} %collective-permute-done.5) | data formatting | bytes 1048576 | tf_op jit(solution)/shard_map/ppermute | solution.py:27
  162.8 2.3 %collective-permute-start.6 = (f32[64,2,8,2]{0,3,2,1:T(2,128)S(1)}, f32[64,2,8,2]{0,3,2,1:T(2,128)S(1)}, u32[]{:S(2)}, u32[]{:S(2)}) collective-permute-start(f32[64,2,8,2]{0,3,2,1:T(2,128)S(1)} %get-tuple-element.9), channel_id=1, source_target_pairs={{0,1},{1,0},{2,3},{3,2},{4,5},{5,4},{6,7},{7,6},{8,9},{9,8},{10,11... | collective-permute-start | bytes 24584 | tf_op jit(solution)/shard_map/ppermute | solution.py:24
  165.2 1.2 fusion.31
  166.4 2.4 %copy.49 = f32[4,4,64,1,128]{2,1,4,0,3:T(4,128)} copy(f32[4,4,64,1,128]{4,2,1,0,3:T(8,128)} %bitcast.77) | data formatting | bytes 1048576 | tf_op jit(solution)/shard_map/reshape | solution.py:55
  168.8 1.7 pad_maximum_fusion.1
  170.6 2.2 %fusion.4 = f32[64,2,6,514]{0,3,2,1:T(8,128)S(1)} fusion(f32[64,2,8,516]{0,3,2,1:T(8,128)S(1)} %pad_maximum_fusion.1, f32[64,2,8,2]{0,3,2,1:T(2,128)S(1)} %collective-permute-done.6, f32[64,2,2,512]{0,3,2,1:T(8,128)S(1)} %copy-done, f32[64,2,4,512]{0,3,2,1:T(8,128)S(1)} %get-tuple-element.7, f32[64,2,2,512]{0,3,2,1:T(8,128)S(1)} %copy.46, ...), kind=kLoop, calls=%fused_computation.13 | loop fusion | flops 5131776 | bytes 8429568 | tf_op jit(solution)/shard_map/sub | solution.py:40
  172.9 1.2 fusion.17
  174.1 3.1 %multiply_reduce_fusion = (f32[]{:T(128)}, f32[64,4096]{1,0:T(8,128)S(1)}) fusion(f32[64,4096]{1,0:T(8,128)S(1)} %copy-done.4, f32[64,4096]{0,1:T(8,128)S(1)} %bitcast.69, f32[64,64]{1,0:T(8,128)S(1)} %fusion.48, f32[]{:T(128)S(6)} %mul.204, f32[64]{0:T(128)S(1)} %gather_fusion.1), kind=kOutput, calls=%fused_computation.62 | convolution fusion | flops 202395648 | bytes 3162376 | tf_op jit(solution)/shard_map/dot_general | solution.py:91
  177.2 37.1 %psum.31 = f32[]{:T(128)} all-reduce(f32[]{:T(128)} %get-tuple-element.17), channel_id=1, replica_groups=mesh['gx'=16,'gy'=2] {'gx','gy'}, use_global_device_ids=true, to_apply=%region_11.12 | all-reduce | flops 1 | bytes 8 | tf_op jit(solution)/shard_map/psum | solution.py:61
  215.0 1.9 copy.60
  216.9 3.2 %add.157 = f32[64,2,4,512]{0,3,2,1:T(8,128)} add(f32[64,2,4,512]{0,3,2,1:T(8,128)S(1)} %copy-done.2, f32[64,2,4,512]{0,3,2,1:T(8,128)} %bitcast.68) | non-fusion elementwise | flops 262144 | bytes 3145728 | tf_op jit(solution)/shard_map/add | solution.py:106
  220.1 2.7 %copy.52 = f32[64,2,4,512]{3,2,1,0:T(4,128)} copy(f32[64,2,4,512]{0,3,2,1:T(8,128)} %add.157) | data formatting | bytes 2097152 | tf_op jit(solution)/shard_map/add | solution.py:106
  (56 shorter events, 7.9 us)
Async XLA Ops:
  0.0 2.8 %copy-start.7 = (f32[2,4,512]{2,1,0:T(4,128)S(1)}, f32[2,4,512]{2,1,0:T(4,128)}, u32[]{:S(2)}) copy-start(f32[2,4,512]{2,1,0:T(4,128)} %param.7) | copy-start | bytes 49156
  8.5 61.1 %collective-permute-start = (f32[64,2,2,512]{3,0,2,1:T(8,128)}, f32[64,2,2,512]{3,0,2,1:T(8,128)}, u32[]{:S(2)}, u32[]{:S(2)}) collective-permute-start(f32[64,2,2,512]{3,0,2,1:T(8,128)} %copy.32), channel_id=1, source_target_pairs={{0,2},{2,4},{4,6},{6,8},{8,10},{10,12},{12,14},{14,16},{16,18},{18... | collective-permute-start | bytes 1572872 | tf_op jit(solution)/shard_map/ppermute | solution.py:24
  10.1 60.8 %collective-permute-start.1 = (f32[64,2,2,512]{3,0,2,1:T(8,128)}, f32[64,2,2,512]{3,0,2,1:T(8,128)}, u32[]{:S(2)}, u32[]{:S(2)}) collective-permute-start(f32[64,2,2,512]{3,0,2,1:T(8,128)} %copy.33), channel_id=1, source_target_pairs={{2,0},{4,2},{6,4},{8,6},{10,8},{12,10},{14,12},{16,14},{18,16},{20... | collective-permute-start | bytes 1572872 | tf_op jit(solution)/shard_map/ppermute | solution.py:27
  16.9 3.6 %copy-start.8 = (s32[16,1,128]{2,1,0:T(1,128)S(1)}, s32[16,1,128]{2,1,0:T(1,128)}, u32[]{:S(2)}) copy-start(s32[16,1,128]{2,1,0:T(1,128)} %param.9) | copy-start | bytes 24580
  23.0 41.5 %copy-start.9 = (s32[1,128]{1,0:T(1,128)S(1)}, s32[1,128]{1,0:T(1,128)}, u32[]{:S(2)}) copy-start(s32[1,128]{1,0:T(1,128)} %param.8) | copy-start | bytes 1540
  61.6 4.5 %copy-start.10 = (f32[1,128]{1,0:T(1,128)S(1)}, f32[1,128]{1,0:T(1,128)}, u32[]{:S(2)}) copy-start(f32[1,128]{1,0:T(1,128)} %param.11) | copy-start | bytes 1540
  61.6 4.5 %copy-start.11 = (f32[1,128]{1,0:T(1,128)S(1)}, f32[1,128]{1,0:T(1,128)}, u32[]{:S(2)}) copy-start(f32[1,128]{1,0:T(1,128)} %param.10) | copy-start | bytes 1540
  74.0 6.0 %collective-permute-start.2 = (f32[64,2,8,2]{0,3,2,1:T(2,128)S(1)}, f32[64,2,8,2]{0,3,2,1:T(2,128)S(1)}, u32[]{:S(2)}, u32[]{:S(2)}) collective-permute-start(f32[64,2,8,2]{0,3,2,1:T(2,128)S(1)} %get-tuple-element.11), channel_id=1, source_target_pairs={{0,1},{1,0},{2,3},{3,2},{4,5},{5,4},{6,7},{7,6},{8,9},{9,8},{10,11... | collective-permute-start | bytes 24584 | tf_op jit(solution)/shard_map/ppermute | solution.py:24
  76.4 3.7 %collective-permute-start.3 = (f32[64,2,8,2]{0,3,2,1:T(2,128)S(1)}, f32[64,2,8,2]{0,3,2,1:T(2,128)S(1)}, u32[]{:S(2)}, u32[]{:S(2)}) collective-permute-start(f32[64,2,8,2]{0,3,2,1:T(2,128)S(1)} %get-tuple-element.12), channel_id=1, source_target_pairs={{1,0},{0,1},{3,2},{2,3},{5,4},{4,5},{7,6},{6,7},{9,8},{8,9},{11,10... | collective-permute-start | bytes 24584 | tf_op jit(solution)/shard_map/ppermute | solution.py:27
  80.1 1.8 copy-start.1
  81.9 2.3 %copy-start.6 = (f32[4,4,64,1,128]{2,1,4,0,3:T(4,128)S(1)}, f32[4,4,64,1,128]{2,1,4,0,3:T(4,128)}, u32[]{:S(2)}) copy-start(f32[4,4,64,1,128]{2,1,4,0,3:T(4,128)} %copy.38) | copy-start | bytes 1572868
  84.2 1.2 copy-start.3
  142.3 16.0 %collective-permute-start.4 = (f32[64,2,2,512]{3,0,2,1:T(8,128)}, f32[64,2,2,512]{3,0,2,1:T(8,128)}, u32[]{:S(2)}, u32[]{:S(2)}) collective-permute-start(f32[64,2,2,512]{3,0,2,1:T(8,128)} %copy.44), channel_id=1, source_target_pairs={{0,2},{2,4},{4,6},{6,8},{8,10},{10,12},{12,14},{14,16},{16,18},{18... | collective-permute-start | bytes 1572872 | tf_op jit(solution)/shard_map/ppermute | solution.py:24
  143.4 16.2 %collective-permute-start.5 = (f32[64,2,2,512]{3,0,2,1:T(8,128)}, f32[64,2,2,512]{3,0,2,1:T(8,128)}, u32[]{:S(2)}, u32[]{:S(2)}) collective-permute-start(f32[64,2,2,512]{3,0,2,1:T(8,128)} %copy.45), channel_id=1, source_target_pairs={{2,0},{4,2},{6,4},{8,6},{10,8},{12,10},{14,12},{16,14},{18,16},{20... | collective-permute-start | bytes 1572872 | tf_op jit(solution)/shard_map/ppermute | solution.py:27
  162.8 6.0 %collective-permute-start.6 = (f32[64,2,8,2]{0,3,2,1:T(2,128)S(1)}, f32[64,2,8,2]{0,3,2,1:T(2,128)S(1)}, u32[]{:S(2)}, u32[]{:S(2)}) collective-permute-start(f32[64,2,8,2]{0,3,2,1:T(2,128)S(1)} %get-tuple-element.9), channel_id=1, source_target_pairs={{0,1},{1,0},{2,3},{3,2},{4,5},{5,4},{6,7},{7,6},{8,9},{9,8},{10,11... | collective-permute-start | bytes 24584 | tf_op jit(solution)/shard_map/ppermute | solution.py:24
  165.1 3.7 %collective-permute-start.7 = (f32[64,2,8,2]{0,3,2,1:T(2,128)S(1)}, f32[64,2,8,2]{0,3,2,1:T(2,128)S(1)}, u32[]{:S(2)}, u32[]{:S(2)}) collective-permute-start(f32[64,2,8,2]{0,3,2,1:T(2,128)S(1)} %get-tuple-element.10), channel_id=1, source_target_pairs={{1,0},{0,1},{3,2},{2,3},{5,4},{4,5},{7,6},{6,7},{9,8},{8,9},{11,10... | collective-permute-start | bytes 24584 | tf_op jit(solution)/shard_map/ppermute | solution.py:27
  168.8 1.8 copy-start
  170.6 2.3 %copy-start.5 = (f32[4,4,64,1,128]{2,1,4,0,3:T(4,128)S(1)}, f32[4,4,64,1,128]{2,1,4,0,3:T(4,128)}, u32[]{:S(2)}) copy-start(f32[4,4,64,1,128]{2,1,4,0,3:T(4,128)} %copy.49) | copy-start | bytes 1572868
  172.9 1.2 copy-start.4
  215.0 1.9 copy-start.2
where the time goes:
time: 225 us; the launch traced here: 223 us
  blocking collectives  117 us (52%)
  local copies, waits for them, and re-layouts  40.5 us (18%)
  matrix products  23.9 us (11%)
  other arithmetic  23.2 us (10%)
  starting transfers between devices  14.7 us (7%)
  between operations  3.04 us (1%)
    psum x1, blocking collectives, per_device(): lax.psum((jnp.dot(flat_dev, drift.T, precision=highest), jnp.dot(drift, d...  41.7 us
    psum x1, blocking collectives, per_device(): lax.psum(jnp.dot(flat_dev, flat_dev.T, precision=highest), ('gx', 'gy'))  38.5 us
    psum x1, blocking collectives, norm_scale(): total = lax.psum(jnp.sum(drift * drift), ('gx', 'gy'))  37.1 us
    ppermute x4, starting transfers between devices, with_halo(): lax.ppermute(lax.slice_in_dim(block, 0, width, axis=dim), axis, backward)  9.55 us
    slice x4, local copies, waits for them, and re-layouts, with_halo(): lax.slice_in_dim(block, block.shape[dim] - width, None, axis=dim)  6.94 us
    dot_general x2, matrix products, per_device(): pulled = jnp.dot(kernel, flat_dev, precision=highest)  6.87 us
    sub x2, other arithmetic, per_device(): deviation = state - background[None]  5.68 us
    dot_general x2, matrix products, per_device(): attract = jnp.dot(kernel, flat_grad, precision=highest)  5.51 us
  transfers between devices with their start and end apart: 8, of which 2 were waited for; matrix products, arithmetic and copies ran while one was open for 17% of the time, Pallas kernels for 0%

commit v1 on v0

v1 whole, which is shorter than its diff:
```python
import functools

import jax
import jax.numpy as jnp
from jax import lax
from jax.experimental import pallas as pl
from jax.experimental.pallas import tpu as pltpu
from jax.sharding import PartitionSpec as P

TILE = 4
CHUNK = 16
LANES = 128
lap_weight = 0.25
prior_weight = 0.05
couple_weight = 0.5
step_length = 1.0
epsilon = 1e-06
highest = lax.Precision.HIGHEST
MESH = pl.DeviceIdType.MESH
F32 = jnp.float32
BF16 = jnp.bfloat16


def split(x):
    high = x.astype(BF16)
    return high, (x - high.astype(F32)).astype(BF16)


def dot_nn(a, b, precision=None):
    return lax.dot_general(
        a, b, (((1,), (0,)), ((), ())), precision=precision, preferred_element_type=F32
    )


def dot_nt(a, b, precision=None):
    return lax.dot_general(
        a, b, (((1,), (1,)), ((), ())), precision=precision, preferred_element_type=F32
    )


def total(x):
    return jnp.sum(jnp.sum(x, axis=1, keepdims=True), axis=0, keepdims=True)


def kernel(
    n_gx, n_gy, size,
    state, background, tile, mask, values, variance,
    out,
    fld, hf, xl, xh, yp, yr, dl, dh, hmat, gpart, grecv, gres, gsum, spart, srecv, small,
    send, recv, gsend, grsem, asend, arsem, ssend, srsem,
):
    layers, rows, count, cols = state.shape
    chunks = count // CHUNK
    n_dev = n_gx * n_gy
    gx = lax.axis_index("gx")
    gy = lax.axis_index("gy")
    up = lax.rem(gx + 1, n_gx)
    down = lax.rem(gx + n_gx - 1, n_gx)
    side = lax.rem(gy + 1, n_gy)
    me = gx * n_gy + gy

    def device(offset):
        other = lax.rem(me + offset, n_dev)
        return other, (lax.div(other, n_gy), lax.rem(other, n_gy))

    barrier = pltpu.get_barrier_semaphore()

    def greet(offset, carry):
        pl.semaphore_signal(barrier, inc=1, device_id=device(offset)[1], device_id_type=MESH)
        return carry

    lax.fori_loop(1, n_dev, greet, 0)

    lane = lax.broadcasted_iota(jnp.int32, (CHUNK, LANES), 1)

    def pack(f, l, r, ps):
        yp[f, l, r, ps, :] = jnp.where(
            lane < LANES // 2,
            fld[f, l, r, ps, pl.ds(0, LANES)],
            fld[f, l, r, ps, pl.ds(cols - LANES, LANES)],
        )

    def copies(f, c):
        ps = pl.ds(pl.multiple_of(c * CHUNK, CHUNK), CHUNK)
        pairs = (
            (fld.at[f, :, pl.ds(rows - 2, 2), ps, :], xl.at[f, :, :, ps, :], (up, gy)),
            (fld.at[f, :, pl.ds(0, 2), ps, :], xh.at[f, :, :, ps, :], (down, gy)),
            (yp.at[f, :, :, ps, :], yr.at[f, :, :, ps, :], (gx, side)),
            (yp.at[f, :, rows - 1, ps, :], dl.at[f, :, ps, :], (up, side)),
            (yp.at[f, :, 0, ps, :], dh.at[f, :, ps, :], (down, side)),
        )
        return [
            pltpu.make_async_remote_copy(
                src_ref=source,
                dst_ref=target,
                send_sem=send.at[f, kind, c],
                recv_sem=recv.at[f, kind, c],
                device_id=where,
                device_id_type=MESH,
            )
            for kind, (source, target, where) in enumerate(pairs)
        ]

    def prior(f, c, emit):
        ps = pl.ds(pl.multiple_of(c * CHUNK, CHUNK), CHUNK)
        for r in range(rows):
            for l in range(layers):
                def row(k):
                    if k < 0:
                        return xl[f, l, k + 2, ps, :]
                    if k >= rows:
                        return xh[f, l, k - rows, ps, :]
                    return fld[f, l, k, ps, :]

                def edge(k):
                    if k < 0:
                        return dl[f, l, ps, :]
                    if k >= rows:
                        return dh[f, l, ps, :]
                    return yr[f, l, k, ps, :]

                here = row(r)
                near = row(r - 1) + row(r + 1)
                far = row(r - 2) + row(r + 2)
                wide = 0.125 * near - here
                edge_here = edge(r)
                edge_wide = 0.125 * (edge(r - 1) + edge(r + 1)) - edge_here

                def shifted(x, e, by):
                    left = pltpu.roll(x, by, 1)
                    first = jnp.where(lane < by, pltpu.roll(e, by, 1), left[:, :LANES])
                    left = jnp.concatenate([first, left[:, LANES:]], axis=1)
                    right = pltpu.roll(x, cols - by, 1)
                    last = jnp.where(
                        lane >= LANES - by, pltpu.roll(e, LANES - by, 1), right[:, cols - LANES :]
                    )
                    right = jnp.concatenate([right[:, : cols - LANES], last], axis=1)
                    return left + right

                curved = 4.25 * here - near + 0.0625 * (far + shifted(here, edge_here, 2))
                curved = curved + shifted(wide, edge_wide, 1)
                other = fld[f, 1 - l, r, ps, :]
                emit(l, r, ps, -prior_weight * (curved + couple_weight * (here - other)))

    def begin(c, carry):
        ps = pl.ds(pl.multiple_of(c * CHUNK, CHUNK), CHUNK)
        for l in range(layers):
            for r in range(rows):
                fld[0, l, r, ps, :] = state[l, r, ps, :] - background[l, pl.ds(r, 1), :]
                pack(0, l, r, ps)
        return carry

    lax.fori_loop(0, chunks, begin, 0)
    pl.semaphore_wait(barrier, n_dev - 1)

    def send_first(c, carry):
        for copy in copies(0, c):
            copy.start()
        return carry

    lax.fori_loop(0, chunks, send_first, 0)

    n_obs = tile.shape[1]
    column = lax.broadcasted_iota(jnp.int32, (cols, n_obs), 0)
    hit = lax.div(column, TILE) == tile[...]
    for r in range(rows):
        weights = 0.25 * mask[pl.ds(r * TILE, TILE), :].astype(F32)
        weights = jnp.concatenate([weights, weights], axis=0)
        weights = jnp.concatenate([weights] * (cols // (2 * TILE)), axis=0)
        hmat[r] = jnp.where(hit, weights, 0.0).astype(BF16)

    def mapped_of(upper):
        acc = jnp.zeros((2 * count, n_obs), F32)
        for r in range(rows):
            acc = acc + dot_nn(jnp.concatenate(split(upper(r)), axis=0), hmat[r])
        return acc[:count] + acc[count:]

    def spread_of(innovation, emit):
        both = jnp.concatenate(split(innovation), axis=0)
        for r in range(rows):
            back = dot_nt(both, hmat[r])
            emit(r, back[:count] + back[count:])

    def put_obs(r, x):
        hf[0, r] = x

    mapped = mapped_of(lambda r: state[0, r])
    spread_of((values[...] - mapped) / variance[...], put_obs)

    def gradient(c, carry):
        for copy in copies(0, c):
            copy.wait_recv()

        def emit(l, r, ps, x):
            fld[1, l, r, ps, :] = x + hf[0, r, ps, :] if l == 0 else x
            pack(1, l, r, ps)

        prior(0, c, emit)
        for copy in copies(1, c):
            copy.start()
        return carry

    lax.fori_loop(0, chunks, gradient, 0)

    same = jnp.zeros((2 * count, 2 * count), F32)
    cross = jnp.zeros((2 * count, 2 * count), F32)
    for l in range(layers):
        for r in range(rows):
            high, low = split(jnp.concatenate([fld[0, l, r], fld[1, l, r]], axis=0))
            same = same + dot_nt(high, high)
            cross = cross + dot_nt(high, low)
    gram = same + cross + cross.T
    share = gpart.shape[1]
    owners = 2 * count // share
    for o in range(owners):
        gpart[o] = gram[o * share : (o + 1) * share]
    if owners < n_dev:
        gpart[pl.ds(owners, n_dev - owners)] = jnp.zeros((n_dev - owners, share, 2 * count), F32)

    def scatter(k):
        other, where = device(k)
        return pltpu.make_async_remote_copy(
            src_ref=gpart.at[other], dst_ref=grecv.at[k], send_sem=gsend.at[k],
            recv_sem=grsem.at[k], device_id=where, device_id_type=MESH,
        )

    def gather(k):
        other, where = device(k)
        return pltpu.make_async_remote_copy(
            src_ref=gsum, dst_ref=gres.at[me], send_sem=asend.at[k],
            recv_sem=arsem.at[k], device_id=where, device_id_type=MESH,
        )

    def share_out(k):
        other, where = device(k)
        return pltpu.make_async_remote_copy(
            src_ref=spart, dst_ref=srecv.at[k], send_sem=ssend.at[k],
            recv_sem=srsem.at[k], device_id=where, device_id_type=MESH,
        )

    def each(make, act):
        def step(k, carry):
            act(make(k))
            return carry

        lax.fori_loop(1, n_dev, step, 0)

    each(scatter, lambda copy: copy.start())

    mapped = mapped_of(lambda r: fld[1, 0, r])
    spread_of(-mapped / variance[...], put_obs)

    grecv[0] = gpart[me]
    each(scatter, lambda copy: copy.wait_recv())
    gsum[...] = jnp.sum(grecv[...], axis=0)
    gres[me] = gsum[...]
    each(gather, lambda copy: copy.start())

    def second(c, carry):
        for copy in copies(1, c):
            copy.wait_recv()

        def emit(l, r, ps, x):
            hf[l, r, ps, :] = x + hf[0, r, ps, :] if l == 0 else x

        prior(1, c, emit)
        return carry

    lax.fori_loop(0, chunks, second, 0)

    each(gather, lambda copy: copy.wait_recv())
    gram = jnp.concatenate([gres[o] for o in range(owners)], axis=0)
    eye = (
        lax.broadcasted_iota(jnp.int32, (count, count), 0)
        == lax.broadcasted_iota(jnp.int32, (count, count), 1)
    ).astype(F32)

    def mixing(matrix):
        diagonal = matrix * eye
        distance = (
            jnp.sum(diagonal, axis=1, keepdims=True)
            + jnp.sum(diagonal, axis=0, keepdims=True)
            - 2.0 * matrix
        )
        width = total(distance * (1.0 - eye)) / (count * (count - 1.0) * size) + epsilon
        weight = jnp.exp(-distance / (2.0 * width * size))
        pull = (jnp.sum(weight, axis=1, keepdims=True) * eye - weight) / (width * count)
        return weight / count, pull

    dev_gram = gram[:count, :count]
    attract, pull = mixing(dev_gram)
    small[0] = jnp.concatenate([pull, attract], axis=1)
    weights = small[0]
    small[1] = dot_nn(weights, gram, highest)
    partial = small[1]
    square = dot_nt(partial, weights, highest)
    crossed = dot_nt(gram[:count], weights, highest)
    small[2] = jnp.concatenate([square, crossed], axis=1)
    square = small[2, :, pl.ds(0, count)]
    crossed = small[2, :, pl.ds(count, count)]
    scale = step_length / jnp.sqrt(total(square * eye) / (count * size) + epsilon)
    next_gram = dev_gram + scale * (crossed + partial[:, :count]) + scale * scale * square
    attract_next, pull_next = mixing(next_gram)
    products = scale * dot_nn(jnp.concatenate([attract_next, pull_next], axis=0), weights, highest)
    on_dev = pull_next + products[count:, :count]
    on_grad = attract_next + products[:count, :count] + products[count:, count:]
    on_second = products[:count, count:]
    zero = jnp.zeros((count, count), F32)
    left = jnp.concatenate(
        [
            jnp.concatenate([on_dev, on_grad, on_second], axis=1),
            jnp.concatenate([scale * pull, scale * attract, zero], axis=1),
        ],
        axis=0,
    )
    left_high, left_low = split(left)
    left_both = jnp.concatenate([left_high, left_low], axis=0)
    sums = jnp.zeros((count, cols), F32)
    for l in range(layers):
        for r in range(rows):
            high, low = split(jnp.concatenate([fld[0, l, r], fld[1, l, r], hf[l, r]], axis=0))
            main = dot_nn(left_both, high)
            mixed = main[: 2 * count] + main[2 * count :] + dot_nn(left_high, low)
            drift = mixed[:count]
            hf[l, r] = drift
            out[l, r] = state[l, r] + mixed[count:]
            sums = sums + drift * drift
    sums = jnp.sum(sums, axis=0, keepdims=True)
    folded = sums[:, :LANES]
    for k in range(1, cols // LANES):
        folded = folded + sums[:, k * LANES : (k + 1) * LANES]
    spart[...] = folded
    srecv[0] = folded
    each(share_out, lambda copy: copy.start())
    each(share_out, lambda copy: copy.wait_recv())
    whole = total(jnp.sum(srecv[...], axis=0))
    scale_next = step_length / jnp.sqrt(whole / (count * size) + epsilon)
    for l in range(layers):
        for r in range(rows):
            out[l, r] = out[l, r] + scale_next * hf[l, r]

    def drain(c, carry):
        for f in range(2):
            for copy in copies(f, c):
                copy.wait_send()
        return carry

    lax.fori_loop(0, chunks, drain, 0)
    each(scatter, lambda copy: copy.wait_send())
    each(gather, lambda copy: copy.wait_send())
    each(share_out, lambda copy: copy.wait_send())


def per_device(n_gx, n_gy, particles, background, obs_tile, obs_mask, obs_value, obs_var):
    count, layers, rows, cols = particles.shape
    assert rows == TILE and n_gy == 2 and count % CHUNK == 0
    n_dev = n_gx * n_gy
    size = float(layers * rows * cols * n_dev)
    n_obs = obs_tile.shape[1]
    share = max(1, 2 * count // n_dev)
    chunks = count // CHUNK
    dma = pltpu.SemaphoreType.DMA
    planes = particles.transpose(1, 2, 0, 3)
    vmem = pl.BlockSpec(memory_space=pltpu.VMEM)
    result = pl.pallas_call(
        functools.partial(kernel, n_gx, n_gy, size),
        out_shape=jax.ShapeDtypeStruct((layers, rows, count, cols), F32),
        in_specs=[vmem] * 6,
        out_specs=vmem,
        scratch_shapes=[
            pltpu.VMEM((2, layers, rows, count, cols), F32),
            pltpu.VMEM((layers, rows, count, cols), F32),
            pltpu.VMEM((2, layers, 2, count, cols), F32),
            pltpu.VMEM((2, layers, 2, count, cols), F32),
            pltpu.VMEM((2, layers, rows, count, LANES), F32),
            pltpu.VMEM((2, layers, rows, count, LANES), F32),
            pltpu.VMEM((2, layers, count, LANES), F32),
            pltpu.VMEM((2, layers, count, LANES), F32),
            pltpu.VMEM((rows, cols, n_obs), BF16),
            pltpu.VMEM((n_dev, share, 2 * count), F32),
            pltpu.VMEM((n_dev, share, 2 * count), F32),
            pltpu.VMEM((n_dev, share, 2 * count), F32),
            pltpu.VMEM((share, 2 * count), F32),
            pltpu.VMEM((1, LANES), F32),
            pltpu.VMEM((n_dev, 1, LANES), F32),
            pltpu.VMEM((3, count, 2 * count), F32),
            dma((2, 5, chunks)),
            dma((2, 5, chunks)),
        ]
        + [dma((n_dev,))] * 6,
        compiler_params=pltpu.CompilerParams(
            collective_id=0, has_side_effects=True, vmem_limit_bytes=48 * 2**20
        ),
    )(planes, background, obs_tile, obs_mask[:, 0], obs_value, obs_var)
    return result.transpose(2, 0, 1, 3)


def solution(mesh):
    n_gx, n_gy = mesh.shape["gx"], mesh.shape["gy"]
    return jax.shard_map(
        functools.partial(per_device, n_gx, n_gy),
        mesh=mesh,
        in_specs=(
            P(None, None, "gx", "gy"),
            P(None, "gx", "gy"),
            P("gx", "gy"),
            P(None, "gx", "gy"),
            P("gx", "gy"),
            P("gx", "gy"),
        ),
        out_specs=P(None, None, "gx", "gy"),
        check_vma=False,
    )
```

time: 225 us -> 54.2 us (0.24)
  blocking collectives: 117 us -> 0 us
  Pallas kernels: 0 us -> 49.9 us
  local copies, waits for them, and re-layouts: 40.5 us -> 4.15 us
  matrix products: 23.9 us -> 0 us
  other arithmetic: 23.2 us -> 0 us
  starting transfers between devices: 14.7 us -> 0 us
  between operations: 3.04 us -> 0.05 us
    psum x3 -> x0, blocking collectives: 117 us -> none  [the longest x1 41.7 us: per_device(): lax.psum((jnp.dot(flat_dev, drift.T, precision=highest), jnp.dot(drift, d...]
    pallas_call x0 -> x1, Pallas kernels: none -> 49.9 us  [per_device(): pl.pallas_call(functools.partial(kernel, n_gx, n_gy, size), out_shape=jax...]
    dot_general x11 -> x0, matrix products: 23.9 us -> none  [the longest x2 6.87 us: per_device(): pulled = jnp.dot(kernel, flat_dev, precision=highest)]
    ppermute x8 -> x0, starting transfers between devices: 14.7 us -> none  [the longest x4 9.55 us: with_halo(): lax.ppermute(lax.slice_in_dim(block, 0, width, axis=dim), axis, backward)]
    slice x9 -> x0, local copies, waits for them, and re-layouts: 13.7 us -> none  [the longest x4 6.94 us: with_halo(): lax.slice_in_dim(block, block.shape[dim] - width, None, axis=dim)]
    sub x4 -> x0, other arithmetic: 10.2 us -> none  [the longest x2 5.68 us: per_device(): deviation = state - background[None]]
    ppermute x4 -> x0, local copies, waits for them, and re-layouts: 7.47 us -> none  [the longest x2 4.73 us: with_halo(): lax.ppermute(lax.slice_in_dim(block, 0, width, axis=dim), axis, backward)]
    reshape x4 -> x0, local copies, waits for them, and re-layouts: 5.91 us -> none  [the longest x2 4.73 us: observe_term(): spread.reshape(TILE, TILE, count, tile_rows, tile_cols)]
  transfers between devices with their start and end apart: 8 -> 0, of which waited for: 2 -> 0; matrix products, arithmetic and copies ran while one was open for 17% -> 0% of each run, Pallas kernels for 0% -> 0%
where the time goes in v1:
time: 54.2 us; the launch traced here: 54.1 us
  Pallas kernels  49.9 us (92%)
  local copies, waits for them, and re-layouts  4.15 us (8%)
    pallas_call x1, Pallas kernels, per_device(): pl.pallas_call(functools.partial(kernel, n_gx, n_gy, size), out_shape=jax...  49.9 us
    unnamed x11, local copies, waits for them, and re-layouts  2.51 us
    transpose x1, local copies, waits for them, and re-layouts, per_device(): return result.transpose(2, 0, 1, 3)  1.65 us

profile of v1, /device:TPU:0, one launch (start us, length us, event | category | flops | bytes accessed | tf_op | source)
XLA Modules:
  0.0 54.1 jit_solution(2841544738658911201)
XLA Ops:
  0.0 0.0 copy-start
  0.0 0.0 copy-start.1
  0.0 1.9 %copy.10 = f32[64,2,4,512]{3,0,2,1:T(8,128)S(1)} copy(f32[64,2,4,512]{3,2,1,0:T(4,128)} %param.6) | data formatting | bytes 2097152 | tf_op args[0]
  1.9 0.0 copy-start.2
  1.9 0.0 copy-start.3
  1.9 0.0 copy-start.4
  1.9 0.0 copy-done
  1.9 0.0 copy-done.1
  1.9 0.6 %copy-done.2 = s32[1,128]{1,0:T(1,128)S(1)} copy-done((s32[1,128]{1,0:T(1,128)S(1)}, s32[1,128]{1,0:T(1,128)}, u32[]{:S(2)}) %copy-start.2) | copy-done | bytes 536
  2.5 0.0 copy-done.3
  2.5 0.0 copy-done.4
  2.6 49.9 %shard_map.64 = f32[2,4,64,512]{3,2,1,0:T(8,128)S(1)} custom-call(f32[2,4,64,512]{3,2,1,0:T(8,128)S(1)} %bitcast.6, f32[2,4,512]{2,1,0:T(4,128)S(1)} %copy-done, s32[1,128]{1,0:T(1,128)S(1)} %copy-done.2, s32[16,128]{1,0:T(8,128)S(1)} %bitcast.7, f32[1,128]{1,0:T(1,128)S(1)} %copy-done.3, f32[1,128]{1,0:T(1,128)S(1)} %copy-done.4), custom_call_target="tpu_custom_call" | custom-call | tf_op jit(solution)/shard_map/pallas_call | solution.py:365
  52.4 1.6 %copy.8 = f32[64,2,4,512]{3,2,1,0:T(4,128)} copy(f32[64,2,4,512]{3,0,2,1:T(8,128)S(1)} %bitcast.5) | data formatting | bytes 2097152 | tf_op jit(solution)/shard_map/transpose | solution.py:395
Async XLA Ops:
  0.0 1.9 %copy-start = (f32[2,4,512]{2,1,0:T(4,128)S(1)}, f32[2,4,512]{2,1,0:T(4,128)}, u32[]{:S(2)}) copy-start(f32[2,4,512]{2,1,0:T(4,128)} %background.1) | copy-start | bytes 49156
  0.0 1.9 %copy-start.1 = (s32[16,1,128]{2,1,0:T(1,128)S(1)}, s32[16,1,128]{2,1,0:T(1,128)}, u32[]{:S(2)}) copy-start(s32[16,1,128]{2,1,0:T(1,128)} %param.9) | copy-start | bytes 24580
  1.9 0.7 %copy-start.2 = (s32[1,128]{1,0:T(1,128)S(1)}, s32[1,128]{1,0:T(1,128)}, u32[]{:S(2)}) copy-start(s32[1,128]{1,0:T(1,128)} %tile.1) | copy-start | bytes 1540
  1.9 0.7 %copy-start.3 = (f32[1,128]{1,0:T(1,128)S(1)}, f32[1,128]{1,0:T(1,128)}, u32[]{:S(2)}) copy-start(f32[1,128]{1,0:T(1,128)} %values.1) | copy-start | bytes 1540
  1.9 0.7 %copy-start.4 = (f32[1,128]{1,0:T(1,128)S(1)}, f32[1,128]{1,0:T(1,128)}, u32[]{:S(2)}) copy-start(f32[1,128]{1,0:T(1,128)} %variance.1) | copy-start | bytes 1540

commit v2 on v1

--- a/solution.py
+++ b/solution.py
@@ -9,6 +9,7 @@
 
 TILE = 4
 CHUNK = 16
+SUBLANES = 8
 LANES = 128
 lap_weight = 0.25
 prior_weight = 0.05
@@ -72,12 +73,37 @@
     lax.fori_loop(1, n_dev, greet, 0)
 
     lane = lax.broadcasted_iota(jnp.int32, (CHUNK, LANES), 1)
-
-    def pack(f, l, r, ps):
-        yp[f, l, r, ps, :] = jnp.where(
-            lane < LANES // 2,
-            fld[f, l, r, ps, pl.ds(0, LANES)],
-            fld[f, l, r, ps, pl.ds(cols - LANES, LANES)],
+    lane8 = lax.broadcasted_iota(jnp.int32, (SUBLANES, LANES), 1)
+    groups = CHUNK // SUBLANES
+    zone = LANES // (layers * rows * groups)
+    owner = lax.rem(lax.div(lane8 + zone // 2, zone), LANES // zone)
+
+    def place(l, r, s):
+        return (l * rows + r) * groups + s
+
+    def pack(f, c):
+        packed = None
+        for l in range(layers):
+            for r in range(rows):
+                for s in range(groups):
+                    start = pl.multiple_of(c * CHUNK + s * SUBLANES, SUBLANES)
+                    ps = pl.ds(start, SUBLANES)
+                    ends = jnp.where(
+                        lane8 < LANES // 2,
+                        fld[f, l, r, ps, pl.ds(0, LANES)],
+                        fld[f, l, r, ps, pl.ds(cols - LANES, LANES)],
+                    )
+                    k = place(l, r, s)
+                    if k == 0:
+                        packed = ends
+                    else:
+                        packed = jnp.where(owner == k, pltpu.roll(ends, k * zone, 1), packed)
+        yp[f, c] = packed
+
+    def unpack(packed, l, r):
+        shifts = [place(l, r, s) * zone for s in range(groups)]
+        return jnp.concatenate(
+            [pltpu.roll(packed, LANES - k, 1) if k else packed for k in shifts], axis=0
         )
 
     def copies(f, c):
@@ -85,9 +111,9 @@
         pairs = (
             (fld.at[f, :, pl.ds(rows - 2, 2), ps, :], xl.at[f, :, :, ps, :], (up, gy)),
             (fld.at[f, :, pl.ds(0, 2), ps, :], xh.at[f, :, :, ps, :], (down, gy)),
-            (yp.at[f, :, :, ps, :], yr.at[f, :, :, ps, :], (gx, side)),
-            (yp.at[f, :, rows - 1, ps, :], dl.at[f, :, ps, :], (up, side)),
-            (yp.at[f, :, 0, ps, :], dh.at[f, :, ps, :], (down, side)),
+            (yp.at[f, c], yr.at[f, c], (gx, side)),
+            (yp.at[f, c], dl.at[f, c], (up, side)),
+            (yp.at[f, c], dh.at[f, c], (down, side)),
         )
         return [
             pltpu.make_async_remote_copy(
@@ -103,8 +129,16 @@
 
     def prior(f, c, emit):
         ps = pl.ds(pl.multiple_of(c * CHUNK, CHUNK), CHUNK)
+        below, level, above = dl[f, c], yr[f, c], dh[f, c]
+        edges = [
+            [unpack(below, l, rows - 1)]
+            + [unpack(level, l, r) for r in range(rows)]
+            + [unpack(above, l, 0)]
+            for l in range(layers)
+        ]
         for r in range(rows):
             for l in range(layers):
+
                 def row(k):
                     if k < 0:
                         return xl[f, l, k + 2, ps, :]
@@ -112,19 +146,12 @@
                         return xh[f, l, k - rows, ps, :]
                     return fld[f, l, k, ps, :]
 
-                def edge(k):
-                    if k < 0:
-                        return dl[f, l, ps, :]
-                    if k >= rows:
-                        return dh[f, l, ps, :]
-                    return yr[f, l, k, ps, :]
-
                 here = row(r)
                 near = row(r - 1) + row(r + 1)
                 far = row(r - 2) + row(r + 2)
                 wide = 0.125 * near - here
-                edge_here = edge(r)
-                edge_wide = 0.125 * (edge(r - 1) + edge(r + 1)) - edge_here
+                edge_here = edges[l][r + 1]
+                edge_wide = 0.125 * (edges[l][r] + edges[l][r + 2]) - edge_here
 
                 def shifted(x, e, by):
                     left = pltpu.roll(x, by, 1)
@@ -147,7 +174,7 @@
         for l in range(layers):
             for r in range(rows):
                 fld[0, l, r, ps, :] = state[l, r, ps, :] - background[l, pl.ds(r, 1), :]
-                pack(0, l, r, ps)
+        pack(0, c)
         return carry
 
     lax.fori_loop(0, chunks, begin, 0)
@@ -193,9 +220,9 @@
 
         def emit(l, r, ps, x):
             fld[1, l, r, ps, :] = x + hf[0, r, ps, :] if l == 0 else x
-            pack(1, l, r, ps)
 
         prior(0, c, emit)
+        pack(1, c)
         for copy in copies(1, c):
             copy.start()
         return carry
@@ -250,23 +277,24 @@
     mapped = mapped_of(lambda r: fld[1, 0, r])
     spread_of(-mapped / variance[...], put_obs)
 
+    def second(c, carry):
+        for copy in copies(1, c):
+            copy.wait_recv()
+
+        def emit(l, r, ps, x):
+            hf[l, r, ps, :] = x + hf[0, r, ps, :] if l == 0 else x
+
+        prior(1, c, emit)
+        return carry
+
+    half = chunks // 2
+    lax.fori_loop(0, half, second, 0)
     grecv[0] = gpart[me]
     each(scatter, lambda copy: copy.wait_recv())
     gsum[...] = jnp.sum(grecv[...], axis=0)
     gres[me] = gsum[...]
     each(gather, lambda copy: copy.start())
-
-    def second(c, carry):
-        for copy in copies(1, c):
-            copy.wait_recv()
-
-        def emit(l, r, ps, x):
-            hf[l, r, ps, :] = x + hf[0, r, ps, :] if l == 0 else x
-
-        prior(1, c, emit)
-        return carry
-
-    lax.fori_loop(0, chunks, second, 0)
+    lax.fori_loop(half, chunks, second, 0)
 
     each(gather, lambda copy: copy.wait_recv())
     gram = jnp.concatenate([gres[o] for o in range(owners)], axis=0)
@@ -305,26 +333,30 @@
     on_dev = pull_next + products[count:, :count]
     on_grad = attract_next + products[:count, :count] + products[count:, count:]
     on_second = products[:count, count:]
-    zero = jnp.zeros((count, count), F32)
-    left = jnp.concatenate(
-        [
-            jnp.concatenate([on_dev, on_grad, on_second], axis=1),
-            jnp.concatenate([scale * pull, scale * attract, zero], axis=1),
-        ],
-        axis=0,
+    def mix(parts, fields, emit):
+        high, low = split(jnp.concatenate(parts, axis=1))
+        both = jnp.concatenate([high, low], axis=0)
+        for l in range(layers):
+            for r in range(rows):
+                top, rest = split(jnp.concatenate(fields(l, r), axis=0))
+                main = dot_nn(both, top)
+                emit(l, r, main[:count] + main[count:] + dot_nn(high, rest))
+
+    sums = [jnp.zeros((count, cols), F32)]
+
+    def put_drift(l, r, x):
+        hf[l, r] = x
+        sums[0] = sums[0] + x * x
+
+    def put_middle(l, r, x):
+        out[l, r] = state[l, r] + scale * x
+
+    mix(
+        [on_dev, on_grad, on_second],
+        lambda l, r: [fld[0, l, r], fld[1, l, r], hf[l, r]],
+        put_drift,
     )
-    left_high, left_low = split(left)
-    left_both = jnp.concatenate([left_high, left_low], axis=0)
-    sums = jnp.zeros((count, cols), F32)
-    for l in range(layers):
-        for r in range(rows):
-            high, low = split(jnp.concatenate([fld[0, l, r], fld[1, l, r], hf[l, r]], axis=0))
-            main = dot_nn(left_both, high)
-            mixed = main[: 2 * count] + main[2 * count :] + dot_nn(left_high, low)
-            drift = mixed[:count]
-            hf[l, r] = drift
-            out[l, r] = state[l, r] + mixed[count:]
-            sums = sums + drift * drift
+    sums = sums[0]
     sums = jnp.sum(sums, axis=0, keepdims=True)
     folded = sums[:, :LANES]
     for k in range(1, cols // LANES):
@@ -332,6 +364,7 @@
     spart[...] = folded
     srecv[0] = folded
     each(share_out, lambda copy: copy.start())
+    mix([pull, attract], lambda l, r: [fld[0, l, r], fld[1, l, r]], put_middle)
     each(share_out, lambda copy: copy.wait_recv())
     whole = total(jnp.sum(srecv[...], axis=0))
     scale_next = step_length / jnp.sqrt(whole / (count * size) + epsilon)
@@ -372,10 +405,10 @@
             pltpu.VMEM((layers, rows, count, cols), F32),
             pltpu.VMEM((2, layers, 2, count, cols), F32),
             pltpu.VMEM((2, layers, 2, count, cols), F32),
-            pltpu.VMEM((2, layers, rows, count, LANES), F32),
-            pltpu.VMEM((2, layers, rows, count, LANES), F32),
-            pltpu.VMEM((2, layers, count, LANES), F32),
-            pltpu.VMEM((2, layers, count, LANES), F32),
+            pltpu.VMEM((2, chunks, SUBLANES, LANES), F32),
+            pltpu.VMEM((2, chunks, SUBLANES, LANES), F32),
+            pltpu.VMEM((2, chunks, SUBLANES, LANES), F32),
+            pltpu.VMEM((2, chunks, SUBLANES, LANES), F32),
             pltpu.VMEM((rows, cols, n_obs), BF16),
             pltpu.VMEM((n_dev, share, 2 * count), F32),
             pltpu.VMEM((n_dev, share, 2 * count), F32),

time: 54.2 us -> 51.9 us (0.958)
  Pallas kernels: 49.9 us -> 47.5 us
    pallas_call x1, Pallas kernels: 49.9 us -> 47.5 us  [per_device(): pl.pallas_call(functools.partial(kernel, n_gx, n_gy, size), out_shape=jax...]
where the time goes in v2:
time: 51.9 us; the launch traced here: 51.7 us
  Pallas kernels  47.5 us (92%)
  local copies, waits for them, and re-layouts  4.15 us (8%)
    pallas_call x1, Pallas kernels, per_device(): pl.pallas_call(functools.partial(kernel, n_gx, n_gy, size), out_shape=jax...  47.5 us
    unnamed x11, local copies, waits for them, and re-layouts  2.51 us
    transpose x1, local copies, waits for them, and re-layouts, per_device(): return result.transpose(2, 0, 1, 3)  1.65 us

profile of v2, /device:TPU:0, one launch (start us, length us, event | category | flops | bytes accessed | tf_op | source)
XLA Modules:
  0.0 51.7 jit_solution(549471787295261164)
XLA Ops:
  0.0 0.0 copy-start
  0.0 0.0 copy-start.1
  0.0 1.9 %copy.10 = f32[64,2,4,512]{3,0,2,1:T(8,128)S(1)} copy(f32[64,2,4,512]{3,2,1,0:T(4,128)} %param.6) | data formatting | bytes 2097152 | tf_op args[0]
  1.9 0.0 copy-start.2
  1.9 0.0 copy-start.3
  1.9 0.0 copy-start.4
  1.9 0.0 copy-done
  1.9 0.0 copy-done.1
  1.9 0.6 %copy-done.2 = s32[1,128]{1,0:T(1,128)S(1)} copy-done((s32[1,128]{1,0:T(1,128)S(1)}, s32[1,128]{1,0:T(1,128)}, u32[]{:S(2)}) %copy-start.2) | copy-done | bytes 536
  2.5 0.0 copy-done.3
  2.5 0.0 copy-done.4
  2.6 47.5 %shard_map.64 = f32[2,4,64,512]{3,2,1,0:T(8,128)S(1)} custom-call(f32[2,4,64,512]{3,2,1,0:T(8,128)S(1)} %bitcast.6, f32[2,4,512]{2,1,0:T(4,128)S(1)} %copy-done, s32[1,128]{1,0:T(1,128)S(1)} %copy-done.2, s32[16,128]{1,0:T(8,128)S(1)} %bitcast.7, f32[1,128]{1,0:T(1,128)S(1)} %copy-done.3, f32[1,128]{1,0:T(1,128)S(1)} %copy-done.4), custom_call_target="tpu_custom_call" | custom-call | tf_op jit(solution)/shard_map/pallas_call | solution.py:398
  50.1 1.6 %copy.8 = f32[64,2,4,512]{3,2,1,0:T(4,128)} copy(f32[64,2,4,512]{3,0,2,1:T(8,128)S(1)} %bitcast.5) | data formatting | bytes 2097152 | tf_op jit(solution)/shard_map/transpose | solution.py:428
Async XLA Ops:
  0.0 1.9 %copy-start = (f32[2,4,512]{2,1,0:T(4,128)S(1)}, f32[2,4,512]{2,1,0:T(4,128)}, u32[]{:S(2)}) copy-start(f32[2,4,512]{2,1,0:T(4,128)} %background.1) | copy-start | bytes 49156
  0.0 1.9 %copy-start.1 = (s32[16,1,128]{2,1,0:T(1,128)S(1)}, s32[16,1,128]{2,1,0:T(1,128)}, u32[]{:S(2)}) copy-start(s32[16,1,128]{2,1,0:T(1,128)} %param.9) | copy-start | bytes 24580
  1.9 0.7 %copy-start.2 = (s32[1,128]{1,0:T(1,128)S(1)}, s32[1,128]{1,0:T(1,128)}, u32[]{:S(2)}) copy-start(s32[1,128]{1,0:T(1,128)} %tile.1) | copy-start | bytes 1540
  1.9 0.7 %copy-start.3 = (f32[1,128]{1,0:T(1,128)S(1)}, f32[1,128]{1,0:T(1,128)}, u32[]{:S(2)}) copy-start(f32[1,128]{1,0:T(1,128)} %values.1) | copy-start | bytes 1540
  1.9 0.7 %copy-start.4 = (f32[1,128]{1,0:T(1,128)S(1)}, f32[1,128]{1,0:T(1,128)}, u32[]{:S(2)}) copy-start(f32[1,128]{1,0:T(1,128)} %variance.1) | copy-start | bytes 1540

commit v3 on v2

--- a/solution.py
+++ b/solution.py
@@ -37,6 +37,13 @@
     return lax.dot_general(
         a, b, (((1,), (1,)), ((), ())), precision=precision, preferred_element_type=F32
     )
+
+
+def dot_split(a, b, dot):
+    high, low = split(a)
+    top, rest = split(b)
+    main = dot(jnp.concatenate([high, low], axis=0), top)
+    return main[: a.shape[0]] + main[a.shape[0] :] + dot(high, rest)
 
 
 def total(x):
@@ -223,11 +230,19 @@
 
         prior(0, c, emit)
         pack(1, c)
+        return carry
+
+    def send_second(c, carry):
         for copy in copies(1, c):
             copy.start()
         return carry
 
-    lax.fori_loop(0, chunks, gradient, 0)
+    def both(c, carry):
+        gradient(c, carry)
+        return send_second(c, carry)
+
+    lax.fori_loop(0, chunks // 2, both, 0)
+    lax.fori_loop(chunks // 2, chunks, gradient, 0)
 
     same = jnp.zeros((2 * count, 2 * count), F32)
     cross = jnp.zeros((2 * count, 2 * count), F32)
@@ -273,6 +288,7 @@
         lax.fori_loop(1, n_dev, step, 0)
 
     each(scatter, lambda copy: copy.start())
+    lax.fori_loop(chunks // 2, chunks, send_second, 0)
 
     mapped = mapped_of(lambda r: fld[1, 0, r])
     spread_of(-mapped / variance[...], put_obs)
@@ -287,7 +303,7 @@
         prior(1, c, emit)
         return carry
 
-    half = chunks // 2
+    half = 0
     lax.fori_loop(0, half, second, 0)
     grecv[0] = gpart[me]
     each(scatter, lambda copy: copy.wait_recv())
@@ -319,17 +335,19 @@
     attract, pull = mixing(dev_gram)
     small[0] = jnp.concatenate([pull, attract], axis=1)
     weights = small[0]
-    small[1] = dot_nn(weights, gram, highest)
+    small[1] = dot_split(weights, gram, dot_nn)
     partial = small[1]
-    square = dot_nt(partial, weights, highest)
-    crossed = dot_nt(gram[:count], weights, highest)
+    square = dot_split(partial, weights, dot_nt)
+    crossed = dot_split(gram[:count], weights, dot_nt)
     small[2] = jnp.concatenate([square, crossed], axis=1)
     square = small[2, :, pl.ds(0, count)]
     crossed = small[2, :, pl.ds(count, count)]
     scale = step_length / jnp.sqrt(total(square * eye) / (count * size) + epsilon)
     next_gram = dev_gram + scale * (crossed + partial[:, :count]) + scale * scale * square
     attract_next, pull_next = mixing(next_gram)
-    products = scale * dot_nn(jnp.concatenate([attract_next, pull_next], axis=0), weights, highest)
+    products = scale * dot_split(
+        jnp.concatenate([attract_next, pull_next], axis=0), weights, dot_nn
+    )
     on_dev = pull_next + products[count:, :count]
     on_grad = attract_next + products[:count, :count] + products[count:, count:]
     on_second = products[:count, count:]

time: 51.9 us -> 51.4 us (level)
  no operation moved by 1% of the time
where the time goes in v3:
time: 51.4 us; the launch traced here: 51.3 us
  Pallas kernels  47.1 us (92%)
  local copies, waits for them, and re-layouts  4.15 us (8%)
    pallas_call x1, Pallas kernels, per_device(): pl.pallas_call(functools.partial(kernel, n_gx, n_gy, size), out_shape=jax...  47.1 us
    unnamed x11, local copies, waits for them, and re-layouts  2.51 us
    transpose x1, local copies, waits for them, and re-layouts, per_device(): return result.transpose(2, 0, 1, 3)  1.65 us

profile of v3, /device:TPU:0, one launch (start us, length us, event | category | flops | bytes accessed | tf_op | source)
XLA Modules:
  0.0 51.3 jit_solution(961022070294746669)
XLA Ops:
  0.0 0.0 copy-start
  0.0 0.0 copy-start.1
  0.0 1.9 %copy.10 = f32[64,2,4,512]{3,0,2,1:T(8,128)S(1)} copy(f32[64,2,4,512]{3,2,1,0:T(4,128)} %param.6) | data formatting | bytes 2097152 | tf_op args[0]
  1.9 0.0 copy-start.2
  1.9 0.0 copy-start.3
  1.9 0.0 copy-start.4
  1.9 0.0 copy-done
  1.9 0.0 copy-done.1
  1.9 0.6 %copy-done.2 = s32[1,128]{1,0:T(1,128)S(1)} copy-done((s32[1,128]{1,0:T(1,128)S(1)}, s32[1,128]{1,0:T(1,128)}, u32[]{:S(2)}) %copy-start.2) | copy-done | bytes 536
  2.5 0.0 copy-done.3
  2.5 0.0 copy-done.4
  2.6 47.1 %shard_map.64 = f32[2,4,64,512]{3,2,1,0:T(8,128)S(1)} custom-call(f32[2,4,64,512]{3,2,1,0:T(8,128)S(1)} %bitcast.6, f32[2,4,512]{2,1,0:T(4,128)S(1)} %copy-done, s32[1,128]{1,0:T(1,128)S(1)} %copy-done.2, s32[16,128]{1,0:T(8,128)S(1)} %bitcast.7, f32[1,128]{1,0:T(1,128)S(1)} %copy-done.3, f32[1,128]{1,0:T(1,128)S(1)} %copy-done.4), custom_call_target="tpu_custom_call" | custom-call | tf_op jit(solution)/shard_map/pallas_call | solution.py:416
  49.6 1.6 %copy.8 = f32[64,2,4,512]{3,2,1,0:T(4,128)} copy(f32[64,2,4,512]{3,0,2,1:T(8,128)S(1)} %bitcast.5) | data formatting | bytes 2097152 | tf_op jit(solution)/shard_map/transpose | solution.py:446
Async XLA Ops:
  0.0 1.9 %copy-start = (f32[2,4,512]{2,1,0:T(4,128)S(1)}, f32[2,4,512]{2,1,0:T(4,128)}, u32[]{:S(2)}) copy-start(f32[2,4,512]{2,1,0:T(4,128)} %background.1) | copy-start | bytes 49156
  0.0 1.9 %copy-start.1 = (s32[16,1,128]{2,1,0:T(1,128)S(1)}, s32[16,1,128]{2,1,0:T(1,128)}, u32[]{:S(2)}) copy-start(s32[16,1,128]{2,1,0:T(1,128)} %param.9) | copy-start | bytes 24580
  1.9 0.7 %copy-start.2 = (s32[1,128]{1,0:T(1,128)S(1)}, s32[1,128]{1,0:T(1,128)}, u32[]{:S(2)}) copy-start(s32[1,128]{1,0:T(1,128)} %tile.1) | copy-start | bytes 1540
  1.9 0.7 %copy-start.3 = (f32[1,128]{1,0:T(1,128)S(1)}, f32[1,128]{1,0:T(1,128)}, u32[]{:S(2)}) copy-start(f32[1,128]{1,0:T(1,128)} %values.1) | copy-start | bytes 1540
  1.9 0.7 %copy-start.4 = (f32[1,128]{1,0:T(1,128)S(1)}, f32[1,128]{1,0:T(1,128)}, u32[]{:S(2)}) copy-start(f32[1,128]{1,0:T(1,128)} %variance.1) | copy-start | bytes 1540
